TPU v7x, 512 devices: a whole 4x8x8 slice. The times are simulated.
512 devices in a mesh: occ: 128 (over z_lo, x, y), grp: 4 (over z_hi, core).
Axes of the slice: x: 4, y: 8, z: 8 (z_hi: 2, z_lo: 4; z = z_hi * 4 + z_lo), core: 2. Of those that a mesh axis runs over, the one named last changes fastest.
Arguments:
- slabs: float32 [512, 512, 1024], P(('occ', 'grp')), may hold values from -4 to 4
- occ_energy: float32 [512], replicated, may hold values from -1.5 to -0.3
- vir_energy: float32 [512], replicated, may hold values from 0.1 to 3
- pair_mask: int32 [512, 2], replicated, may hold values from 0 to 1, as said below
Outputs:
- aux_grad: float32 [512, 512, 1024], P(('occ', 'grp'))
- vir_density: float32 [512, 512], P('occ')
Inputs may be any that keep to these rules, and one draw needn't show every extreme that they name: Entries are 0 or 1; orbital 0 is paired with all of its 2 partners, and so is every orbital i >= 512 - 1 - 2 (pair_mask[i, k - 1] = 1 for every 1 <= k <= 2 on those rows).
All inputs are finite; a program needn't handle non-finite values.
Results may differ from a plain program's by a relative error of at most 0.0003.
Values sent between devices are 32-bit elements; how exact they have to be, the bound alone decides.
A program may use at most 128 MiB of HBM per device.

v0:
```python
import jax
import jax.numpy as jnp
from jax import lax
from jax.sharding import PartitionSpec as P

highest = lax.Precision.HIGHEST


def shifted(block, axis, distance):
    devices = range(lax.axis_size(axis))
    route = [(i - distance, i) for i in devices if i - distance in devices]
    return lax.ppermute(block, axis, route)


def pair_terms(left_slab, right_slab, left_energy, right_energy, virtual):
    coulomb = jnp.dot(
        left_slab, right_slab.T, precision=highest, preferred_element_type=jnp.float32
    )
    denominator = left_energy + right_energy - virtual[:, None] - virtual[None, :]
    amplitude = coulomb / denominator
    grad_left = jnp.dot(
        amplitude, right_slab, precision=highest, preferred_element_type=jnp.float32
    )
    grad_right = jnp.dot(
        amplitude.T, left_slab, precision=highest, preferred_element_type=jnp.float32
    )
    density = jnp.dot(amplitude, amplitude.T, precision=highest, preferred_element_type=jnp.float32)
    density = density + jnp.dot(
        amplitude.T, amplitude, precision=highest, preferred_element_type=jnp.float32
    )
    return (grad_left, grad_right, density)


def body(slabs, occ_energy, vir_energy, pair_mask):
    own_slab = slabs[0]
    orbitals = lax.axis_size(("occ", "grp"))
    position = lax.axis_index(("occ", "grp"))
    own_energy = lax.dynamic_index_in_dim(occ_energy, position, 0, keepdims=False)
    grad_left, grad_right, density = pair_terms(
        own_slab, own_slab, own_energy, own_energy, vir_energy
    )
    gradient = grad_left + grad_right
    offsets = pair_mask.shape[1]
    for offset in range(1, offsets + 1):
        column = pair_mask[:, offset - 1]
        partner_index = jnp.minimum(position + offset, orbitals - 1)
        partner_energy = lax.dynamic_index_in_dim(occ_energy, partner_index, 0, keepdims=False)
        forward_flag = lax.dynamic_index_in_dim(column, position, 0, keepdims=False)
        forward_active = (forward_flag == 1) & (position + offset < orbitals)
        partner_slab = shifted(own_slab, ("occ", "grp"), -offset)

        def whole_pair():
            return pair_terms(own_slab, partner_slab, own_energy, partner_energy, vir_energy)

        def empty_pair():
            return (jnp.zeros_like(own_slab), jnp.zeros_like(own_slab), jnp.zeros_like(density))

        grad_left, grad_right, term = lax.cond(forward_active, whole_pair, empty_pair)
        returned = shifted(grad_right, ("occ", "grp"), offset)
        gradient = gradient + grad_left + returned
        density = density + term
    row_count = density.shape[0] // lax.axis_size("occ")
    summed = lax.psum(density, ("occ", "grp"))
    own_rows = lax.dynamic_slice_in_dim(summed, lax.axis_index("occ") * row_count, row_count, 0)
    return (gradient[None], own_rows / orbitals)


def solution(mesh):
    placed = (P(("occ", "grp"), None, None), P(), P(), P())
    return jax.shard_map(
        body,
        mesh=mesh,
        in_specs=placed,
        out_specs=(P(("occ", "grp"), None, None), P("occ", None)),
        check_vma=False,
    )
```

profile of v0, /device:TPU:1, one launch (start us, length us, event | category | flops | bytes accessed | tf_op | source)
XLA Modules:
  0.0 633.2 jit_solution(11234347557603762785)
XLA Ops:
  7.2 8.7 %collective-permute-start = (f32[512,1024]{1,0:T(8,128)}, f32[512,1024]{1,0:T(8,128)S(1)}, u32[]{:S(2)}, u32[]{:S(2)}) collective-permute-start(f32[512,1024]{1,0:T(8,128)} %bitcast.34), channel_id=1, source_target_pairs={{1,0},{2,1},{3,2},{4,3},{5,4},{6,5},{7,6},{8,7},{9,8},{10,9},{11,1... | collective-permute-start | bytes 6291464 | tf_op jit(solution)/shard_map/ppermute | solution.py:12
  16.0 1.3 collective-permute-start.2
  17.3 1.3 dynamic_slice.24
  18.6 0.8 fusion.27
  19.3 0.6 fusion.28
  22.5 70.1 %collective-permute-done = f32[512,1024]{1,0:T(8,128)S(1)} collective-permute-done((f32[512,1024]{1,0:T(8,128)}, f32[512,1024]{1,0:T(8,128)S(1)}, u32[]{:S(2)}, u32[]{:S(2)}) %collective-permute-start) | collective-permute-done | bytes 2097184 | tf_op jit(solution)/shard_map/ppermute | solution.py:12
  92.6 2.2 conditional.2
  92.9 1.6 broadcast.20.clone
  94.8 20.0 %collective-permute-start.1 = (f32[512,1024]{1,0:T(8,128)}, f32[512,1024]{1,0:T(8,128)}, u32[]{:S(2)}, u32[]{:S(2)}) collective-permute-start(f32[512,1024]{1,0:T(8,128)} %get-tuple-element.103), channel_id=1, source_target_pairs={{0,1},{1,2},{2,3},{3,4},{4,5},{5,6},{6,7},{7,8},{8,9},{9,10},{10,1... | collective-permute-start | bytes 6291464 | tf_op jit(solution)/shard_map/ppermute | solution.py:12
  114.8 4.5 conditional.3
  114.8 1.6 broadcast.22
  116.4 1.6 broadcast.22.clone
  118.0 1.1 broadcast.23
  119.3 20.1 %collective-permute-start.3 = (f32[512,1024]{1,0:T(8,128)}, f32[512,1024]{1,0:T(8,128)}, u32[]{:S(2)}, u32[]{:S(2)}) collective-permute-start(f32[512,1024]{1,0:T(8,128)} %get-tuple-element.105), channel_id=1, source_target_pairs={{0,2},{1,3},{2,4},{3,5},{4,6},{5,7},{6,8},{7,9},{8,10},{9,11},{10,... | collective-permute-start | bytes 6291464 | tf_op jit(solution)/shard_map/ppermute | solution.py:12
  139.4 0.7 broadcast_subtract_fusion.2
  140.1 5.7 fusion.25
  145.9 2.3 fusion
  148.2 2.2 fusion.12
  150.4 2.7 add_add_fusion
  153.2 6.3 fusion.4
  159.5 5.2 fusion.6
  164.7 452.2 %all-reduce.2.cloned.1.call-done = f32[512,512]{1,0:T(8,128)} async-done(((f32[512,512]{1,0:T(8,128)}), f32[512,512]{1,0:T(8,128)}) %all-reduce.2.cloned.1.call-update) | async-done | bytes 1048592 | tf_op jit(solution)/shard_map/psum | solution.py:63
  616.9 1.3 dynamic-slice_multiply_fusion
  618.2 7.7 %add_bitcast_fusion = f32[1,512,1024]{2,1,0:T(8,128)} fusion(f32[512,1024]{1,0:T(8,128)} %collective-permute-done.3, f32[512,1024]{1,0:T(8,128)} %get-tuple-element.104, f32[512,1024]{1,0:T(8,128)} %collective-permute-done.1, f32[512,1024]{1,0:T(8,128)} %copy-done.3, f32[512,1024]{1,0:T(8,128)} %fusion.6, f32[512,1024]{1,0:T(8,128)} %fusion.4), kind=kLoop, calls=%fused_computation.6 | loop fusion | flops 2621440 | bytes 14680064 | tf_op jit(solution)/shard_map/broadcast_in_dim | solution.py:65
  (17 shorter events, 0.4 us)
Async XLA Ops:
  7.2 609.7 %all-reduce.2.cloned.1.call-start = ((), (), s32[]{:S(2)}) async-start(), calls=%async_computation | async-start | bytes 2097152 | tf_op jit(solution)/shard_map/psum | solution.py:63
  7.2 85.4 %collective-permute-start = (f32[512,1024]{1,0:T(8,128)}, f32[512,1024]{1,0:T(8,128)S(1)}, u32[]{:S(2)}, u32[]{:S(2)}) collective-permute-start(f32[512,1024]{1,0:T(8,128)} %bitcast.34), channel_id=1, source_target_pairs={{1,0},{2,1},{3,2},{4,3},{5,4},{6,5},{7,6},{8,7},{9,8},{10,9},{11,1... | collective-permute-start | bytes 6291464 | tf_op jit(solution)/shard_map/ppermute | solution.py:12
  16.0 98.8 %collective-permute-start.2 = (f32[512,1024]{1,0:T(8,128)}, f32[512,1024]{1,0:T(8,128)}, u32[]{:S(2)}, u32[]{:S(2)}) collective-permute-start(f32[512,1024]{1,0:T(8,128)} %bitcast.35), channel_id=1, source_target_pairs={{2,0},{3,1},{4,2},{5,3},{6,4},{7,5},{8,6},{9,7},{10,8},{11,9},{12,... | collective-permute-start | bytes 6291464 | tf_op jit(solution)/shard_map/ppermute | solution.py:12
  94.8 20.0 %copy-start.3 = (f32[512,1024]{1,0:T(8,128)}, f32[512,1024]{1,0:T(8,128)S(1)}, u32[]{:S(2)}) copy-start(f32[512,1024]{1,0:T(8,128)S(1)} %get-tuple-element.102) | copy-start | bytes 6291460
  94.8 523.4 %collective-permute-start.1 = (f32[512,1024]{1,0:T(8,128)}, f32[512,1024]{1,0:T(8,128)}, u32[]{:S(2)}, u32[]{:S(2)}) collective-permute-start(f32[512,1024]{1,0:T(8,128)} %get-tuple-element.103), channel_id=1, source_target_pairs={{0,1},{1,2},{2,3},{3,4},{4,5},{5,6},{6,7},{7,8},{8,9},{9,10},{10,1... | collective-permute-start | bytes 6291464 | tf_op jit(solution)/shard_map/ppermute | solution.py:12
  119.3 26.5 %copy-start.8 = (f32[512]{0:T(512)S(1)}, f32[512]{0:T(512)}, u32[]{:S(2)}) copy-start(f32[512]{0:T(512)} %param.10) | copy-start | bytes 6148
  119.3 498.9 %collective-permute-start.3 = (f32[512,1024]{1,0:T(8,128)}, f32[512,1024]{1,0:T(8,128)}, u32[]{:S(2)}, u32[]{:S(2)}) collective-permute-start(f32[512,1024]{1,0:T(8,128)} %get-tuple-element.105), channel_id=1, source_target_pairs={{0,2},{1,3},{2,4},{3,5},{4,6},{5,7},{6,8},{7,9},{8,10},{9,11},{10,... | collective-permute-start | bytes 6291464 | tf_op jit(solution)/shard_map/ppermute | solution.py:12
  145.8 2.3 copy-start.4
  150.4 2.8 copy-start
  153.2 6.3 copy-start.5
Sparse Core Ops, SparseCore 0:
  153.3 463.5 all-reduce.1
where the time goes:
time: 644 us; the launch traced here: 633 us
  waiting for transfers between devices  522 us (81%)
  starting transfers between devices  50.2 us (8%)
  matrix products  21.8 us (3%)
  between operations  17.2 us (3%)
  other arithmetic  13 us (2%)
  local copies, waits for them, and re-layouts  8.33 us (1%)
    psum x1, waiting for transfers between devices, body(): summed = lax.psum(density, ('occ', 'grp'))  452 us
    ppermute x4, waiting for transfers between devices, shifted(): return lax.ppermute(block, axis, route)  70.1 us
    ppermute x4, starting transfers between devices, shifted(): return lax.ppermute(block, axis, route)  50.1 us
  transfers between devices with their start and end apart: 5, of which 2 were waited for; matrix products, arithmetic and copies ran while one was open for 6% of the time, Pallas kernels for 0%

commit v1 on v0

v1 whole, which is shorter than its diff:
```python
import functools

import jax
import jax.numpy as jnp
from jax import lax
from jax.experimental import pallas as pl
from jax.experimental.pallas import tpu as pltpu
from jax.sharding import PartitionSpec as P

MESH = pl.DeviceIdType.MESH
V, A, N = 512, 1024, 512
BLOCK = 128
PIECE = 32
PIECES = V // PIECE
PER_BLOCK = BLOCK // PIECE
bf16, f32 = jnp.bfloat16, jnp.float32


def device(x, y, z, core):
    return (lax.rem(z, 4) * 32 + x * 8 + y, (z // 4) * 2 + core)


def split(value):
    high = value.astype(bf16)
    return high, (value - high.astype(f32)).astype(bf16)


def times(left, right):
    return jnp.dot(left, right, preferred_element_type=f32)


def times_t(left, right):
    return lax.dot_general(left, right, (((1,), (1,)), ((), ())), preferred_element_type=f32)


def kernel(
    slab, occ_ref, vir_ref, mask_ref, grad_out, density_out,
    own_high, own_low, own, other, near, grad, half, vir_col,
    rhs_high, rhs_low, t_high, t_low,
    core_in, x_buf, x_in, y_buf, y_in, z_buf, z_in, last_buf, last_in,
    local_sem, o_send, o_recv, z_send, z_recv, y_send, y_recv, p_send, p_recv,
    c_send, c_recv, xs, xr, ys, yr, zs, zr, ls, lr,
):
    occ, grp = lax.axis_index("occ"), lax.axis_index("grp")
    x, y = lax.rem(occ // 8, 4), lax.rem(occ, 8)
    z_low, z_high, core = occ // 32, grp // 2, lax.rem(grp, 2)
    z = z_high * 4 + z_low
    position = occ * 4 + grp
    partner = device(x, y, z, 1 - core)
    antipode = device(x, y, lax.rem(z + 4, 8), core)
    step = 1 - 2 * z_high
    target, source = occ + step, occ - step
    has_target = (target >= 0) & (target < 128)
    has_source = (source >= 0) & (source < 128)
    gives_z = z_high == core

    load = pltpu.make_async_copy(slab.at[0], own, local_sem.at[0])
    load.start()

    def x_peer(k):
        return device(lax.rem(x + k, 4), y, z, core)

    def y_peer(k):
        return device(x, lax.rem(y + k, 8), z, core)

    def z_peer(k):
        return device(x, y, lax.rem(z + k, 8), core)

    barrier = pltpu.get_barrier_semaphore()
    peers = [partner]
    peers += [x_peer(k) for k in range(1, 4)]
    peers += [y_peer(k) for k in range(1, 8)]
    peers += [z_peer(k) for k in range(1, 8)]
    peers += [(lax.rem(occ + k, 128), grp) for k in (1, 127)]
    for peer in peers:
        pl.semaphore_signal(barrier, inc=1, device_id=peer, device_id_type=MESH)
    pl.semaphore_wait(barrier, len(peers))

    def rows(p):
        return pl.ds(pl.multiple_of(p * PIECE, PIECE), PIECE)

    def spot(kind, p):
        start = ((p // PER_BLOCK) * 3 + kind) * BLOCK + lax.rem(p, PER_BLOCK) * PIECE
        return near.at[pl.ds(pl.multiple_of(start, PIECE), PIECE)]

    def remote(src, dst, send, recv, to):
        return pltpu.make_async_remote_copy(
            src_ref=src, dst_ref=dst, send_sem=send, recv_sem=recv, device_id=to, device_id_type=MESH
        )

    def z_copy(p):
        return remote(slab.at[0, rows(p)], spot(0, p), z_send.at[p], z_recv.at[p], antipode)

    def y_copy(p):
        return remote(spot(0, p), spot(2, p), y_send.at[p], y_recv.at[p], (target, grp))

    def p_copy(p, kind):
        return remote(spot(kind, p), spot(1, p), p_send.at[p], p_recv.at[p], partner)

    o_copy = remote(slab.at[0], other, o_send, o_recv, partner)

    def start_z(p, carry):
        z_copy(p).start()
        return carry

    lax.fori_loop(0, PIECES, start_z, 0)
    o_copy.start()

    load.wait()
    vir_row = vir_ref[...]
    vir_col[...] = jnp.transpose(jnp.broadcast_to(vir_row, (128, V)))
    for m in range(4):
        high, low = split(own[pl.ds(m * 128, 128), :])
        own_high[pl.ds(m * 128, 128), :] = high
        own_low[pl.ds(m * 128, 128), :] = low
    grad[...] = jnp.zeros_like(grad)
    half[...] = jnp.zeros_like(half)

    @pl.when(jnp.logical_not(has_source))
    def _():
        for b in range(4):
            near[pl.ds((3 * b + 2) * BLOCK, BLOCK), :] = jnp.zeros((BLOCK, A), f32)

    @pl.when(jnp.logical_not(has_source) & gives_z)
    def _():
        for b in range(4):
            near[pl.ds((3 * b + 1) * BLOCK, BLOCK), :] = jnp.zeros((BLOCK, A), f32)

    own_energy = occ_ref[position]

    def weight_of(other_index):
        low, high = jnp.minimum(position, other_index), jnp.maximum(position, other_index)
        present = (low >= 0) & (high < N)
        flag = mask_ref[jnp.maximum(low, 0), high - low - 1]
        return jnp.where(present & (flag == 1), 1.0, 0.0).astype(f32)

    def energy_of(other_index):
        return occ_ref[jnp.clip(other_index, 0, N - 1)]

    side = 1 - 2 * core
    o_index, x_index = position + side, position - side
    z_index, y_index = position + 2 * step, position - 2 * step
    facts = {
        "own": (own_energy, jnp.float32(2.0)),
        "o": (energy_of(o_index), weight_of(o_index)),
        "z": (energy_of(z_index), weight_of(z_index)),
        "p": (energy_of(x_index), weight_of(x_index)),
        "y": (energy_of(y_index), weight_of(y_index)),
    }

    def block_terms(pieces):
        width = len(pieces) * BLOCK
        for n, (ref, _, _) in enumerate(pieces):
            high, low = split(ref[...])
            rhs_high[pl.ds(n * BLOCK, BLOCK), :] = high
            rhs_low[pl.ds(n * BLOCK, BLOCK), :] = low
        tiles = []
        for _, number, name in pieces:
            energy, weight = facts[name]
            start = pl.multiple_of(number * BLOCK, BLOCK)
            tiles.append((own_energy + energy - vir_ref[:, pl.ds(start, BLOCK)], weight))

        def rows_of(m, carry):
            band = pl.ds(pl.multiple_of(m * 256, 256), 256)
            left_high, left_low = own_high[band, :], own_low[band, :]
            right_high, right_low = rhs_high[:width, :], rhs_low[:width, :]
            coulomb = times_t(left_high, right_high)
            coulomb += times_t(left_high, right_low)
            coulomb += times_t(left_low, right_high)
            column = vir_col[band, :]
            for n, (base, _) in enumerate(tiles):
                cut = slice(n * BLOCK, (n + 1) * BLOCK)
                high, low = split(coulomb[:, cut] / (base - column))
                t_high[band, cut] = high
                t_low[band, cut] = low
            weighted_high = jnp.concatenate(
                [t_high[band, n * BLOCK:(n + 1) * BLOCK] * tiles[n][1].astype(bf16) for n in range(len(tiles))], axis=1
            )
            weighted_low = jnp.concatenate(
                [t_low[band, n * BLOCK:(n + 1) * BLOCK] * tiles[n][1].astype(bf16) for n in range(len(tiles))], axis=1
            )
            grad[band, :] += (
                times(weighted_high, right_high) + times(weighted_high, right_low) + times(weighted_low, right_high)
            )
            return carry

        lax.fori_loop(0, 2, rows_of, 0)

        def density_rows(m, carry):
            band = pl.ds(pl.multiple_of(m * 256, 256), 256)
            weighted_high = jnp.concatenate(
                [t_high[band, n * BLOCK:(n + 1) * BLOCK] * tiles[n][1].astype(bf16) for n in range(len(tiles))], axis=1
            )
            weighted_low = jnp.concatenate(
                [t_low[band, n * BLOCK:(n + 1) * BLOCK] * tiles[n][1].astype(bf16) for n in range(len(tiles))], axis=1
            )
            for h in range(2):
                other_high = t_high[pl.ds(h * 256, 256), :width]
                other_low = t_low[pl.ds(h * 256, 256), :width]
                half[h, band, :] += (
                    times_t(weighted_high, other_high)
                    + times_t(weighted_high, other_low)
                    + times_t(weighted_low, other_high)
                )
            return carry

        lax.fori_loop(0, 2, density_rows, 0)

    def part(ref, b):
        return ref.at[pl.ds(pl.multiple_of(b * BLOCK, BLOCK), BLOCK)]

    def own_blocks(b, carry):
        block_terms([(part(own, 2 * b), 2 * b, "own"), (part(own, 2 * b + 1), 2 * b + 1, "own")])
        return carry

    lax.fori_loop(0, 2, own_blocks, 0)
    o_copy.wait_recv()

    def other_blocks(b, carry):
        block_terms([(part(other, 2 * b), 2 * b, "o"), (part(other, 2 * b + 1), 2 * b + 1, "o")])
        return carry

    lax.fori_loop(0, 2, other_blocks, 0)

    def take(p, carry):
        z_copy(p).wait_recv()

        @pl.when(has_target)
        def _():
            y_copy(p).start()

        @pl.when(gives_z)
        def _():
            p_copy(p, 0).start()

        return carry

    def pass_on(p, carry):
        @pl.when(has_source)
        def _():
            y_copy(p).wait_recv()

            @pl.when(jnp.logical_not(gives_z))
            def _():
                p_copy(p, 2).start()

        return carry

    def near_blocks(b, carry):
        lax.fori_loop(b * PER_BLOCK, (b + 1) * PER_BLOCK, take, 0)
        lax.fori_loop(b * PER_BLOCK, (b + 1) * PER_BLOCK, pass_on, 0)

        def settle(p, carry):
            @pl.when(has_source | jnp.logical_not(gives_z))
            def _():
                p_copy(p, 0).wait_recv()

            return carry

        lax.fori_loop(b * PER_BLOCK, (b + 1) * PER_BLOCK, settle, 0)
        block_terms(
            [(part(near, 3 * b), b, "z"), (part(near, 3 * b + 1), b, "p"), (part(near, 3 * b + 2), b, "y")]
        )
        return carry

    lax.fori_loop(0, 4, near_blocks, 0)
    save = pltpu.make_async_copy(grad, grad_out.at[0], local_sem.at[1])
    save.start()

    c_copy = remote(half.at[1 - core], core_in, c_send, c_recv, partner)
    c_copy.start()
    c_copy.wait_recv()
    for q in range(4):
        for k in range(4):
            rows_k = pl.ds(q * 128 + k * 32, 32)
            x_buf[k, pl.ds(q * 32, 32), :] = half[core, rows_k, :] + core_in[rows_k, :]
    x_copies = [
        remote(x_buf.at[lax.rem(x + k, 4)], x_in.at[k - 1], xs.at[k - 1], xr.at[k - 1], x_peer(k)) for k in range(1, 4)
    ]
    for copy in x_copies:
        copy.start()
    for copy in x_copies:
        copy.wait_recv()
    for q in range(4):
        band = pl.ds(q * 32, 32)
        total = x_buf[x, band, :] + x_in[0, band, :] + x_in[1, band, :] + x_in[2, band, :]
        for k in range(8):
            y_buf[k, pl.ds(q * 4, 4), :] = total[k * 4:(k + 1) * 4, :]
    y_copies = [
        remote(y_buf.at[lax.rem(y + k, 8)], y_in.at[k - 1], ys.at[k - 1], yr.at[k - 1], y_peer(k)) for k in range(1, 8)
    ]
    for copy in y_copies:
        copy.start()
    for copy in y_copies:
        copy.wait_recv()
    total = y_buf[y]
    for k in range(7):
        total += y_in[k]
    for q in range(4):
        z_buf[q, pl.ds(0, 4), :] = total[q * 4:(q + 1) * 4, :]
        z_buf[q, pl.ds(4, 4), :] = jnp.zeros((4, 256), f32)
    z_copies = [
        remote(z_buf.at[lax.rem(z + k, 4)], z_in.at[k - 1], zs.at[k - 1], zr.at[k - 1], z_peer(k)) for k in range(1, 8)
    ]
    for copy in z_copies:
        copy.start()
    for copy in z_copies:
        copy.wait_recv()
    total = z_buf[z_low]
    for k in range(7):
        total += z_in[k]
    total = total * f32(1.0 / N)
    last_buf[...] = total
    l_copy = remote(last_buf, last_in, ls, lr, partner)
    l_copy.start()
    l_copy.wait_recv()

    @pl.when(core == 0)
    def _():
        density_out[:, 0:256] = total[0:4, :]
        density_out[:, 256:512] = last_in[0:4, :]

    @pl.when(core == 1)
    def _():
        density_out[:, 0:256] = last_in[0:4, :]
        density_out[:, 256:512] = total[0:4, :]

    o_copy.wait_send()

    def drain(p, carry):
        z_copy(p).wait_send()

        @pl.when(has_target)
        def _():
            y_copy(p).wait_send()

        @pl.when(gives_z | has_source)
        def _():
            p_copy(p, 0).wait_send()

        return carry

    lax.fori_loop(0, PIECES, drain, 0)
    for copy in [c_copy, *x_copies, *y_copies, *z_copies, l_copy]:
        copy.wait_send()
    save.wait()


def body(slabs, occ_energy, vir_energy, pair_mask):
    dma = pltpu.SemaphoreType.DMA
    vmem = pltpu.VMEM
    smem = pl.BlockSpec(memory_space=pltpu.SMEM)
    whole = pl.BlockSpec(memory_space=pltpu.VMEM)
    anywhere = pl.BlockSpec(memory_space=pl.ANY)
    return pl.pallas_call(
        kernel,
        out_shape=(jax.ShapeDtypeStruct((1, V, A), f32), jax.ShapeDtypeStruct((4, V), f32)),
        in_specs=[anywhere, smem, whole, smem],
        out_specs=(anywhere, whole),
        scratch_shapes=[
            vmem((V, A), bf16), vmem((V, A), bf16), vmem((V, A), f32), vmem((V, A), f32),
            vmem((12 * BLOCK, A), f32), vmem((V, A), f32), vmem((2, V, V // 2), f32), vmem((V, 128), f32),
            vmem((3 * BLOCK, A), bf16), vmem((3 * BLOCK, A), bf16),
            vmem((V, 3 * BLOCK), bf16), vmem((V, 3 * BLOCK), bf16),
            vmem((V, 256), f32), vmem((4, 128, 256), f32), vmem((3, 128, 256), f32),
            vmem((8, 16, 256), f32), vmem((7, 16, 256), f32), vmem((4, 8, 256), f32), vmem((7, 8, 256), f32),
            vmem((8, 256), f32), vmem((8, 256), f32),
            dma((2,)), dma, dma, dma((PIECES,)), dma((PIECES,)), dma((PIECES,)), dma((PIECES,)), dma((PIECES,)),
            dma((PIECES,)), dma, dma, dma((3,)), dma((3,)), dma((7,)), dma((7,)), dma((7,)), dma((7,)), dma, dma,
        ],
        compiler_params=pltpu.CompilerParams(
            collective_id=0, has_side_effects=True, vmem_limit_bytes=60 * 1024 * 1024
        ),
    )(slabs, occ_energy, vir_energy[None, :], pair_mask)


def solution(mesh):
    placed = (P(("occ", "grp"), None, None), P(), P(), P())
    return jax.shard_map(
        body,
        mesh=mesh,
        in_specs=placed,
        out_specs=(P(("occ", "grp"), None, None), P("occ", None)),
        check_vma=False,
    )
```

time: 644 us -> 222 us (0.34); the launches traced: 633 us -> 222 us
  waiting for transfers between devices: 522 us -> 0 us
  Pallas kernels: 0 us -> 216 us
  starting transfers between devices: 50.2 us -> 0 us
  matrix products: 21.8 us -> 0 us
  between operations: 17.2 us -> 0.65 us
  other arithmetic: 13 us -> 0 us
    psum x1 -> x0, waiting for transfers between devices: 452 us -> none  [body(): summed = lax.psum(density, ('occ', 'grp'))]
    pallas_call x0 -> x1, Pallas kernels: none -> 216 us  [body(): pl.pallas_call(kernel, out_shape=(jax.ShapeDtypeStruct((1, V, A), f32), j...]
    ppermute x4 -> x0, waiting for transfers between devices: 70.1 us -> none  [shifted(): return lax.ppermute(block, axis, route)]
    ppermute x4 -> x0, starting transfers between devices: 50.1 us -> none  [shifted(): return lax.ppermute(block, axis, route)]
    dot_general x5 -> x0, matrix products: 21.8 us -> none  [the longest x1 6.27 us: pair_terms(): jnp.dot(amplitude.T, left_slab, precision=highest, preferred_element_type...]
    broadcast_in_dim x1 -> x0, other arithmetic: 7.69 us -> none  [body(): return (gradient[None], own_rows / orbitals)]
  transfers between devices with their start and end apart: 5 -> 0, of which waited for: 2 -> 0; matrix products, arithmetic and copies ran while one was open for 6% -> 0% of each run, Pallas kernels for 0% -> 0%
where the time goes in v1:
time: 222 us
  Pallas kernels  216 us (97%)
  local copies, waits for them, and re-layouts  5.31 us (2%)
    pallas_call x1, Pallas kernels, body(): pl.pallas_call(kernel, out_shape=(jax.ShapeDtypeStruct((1, V, A), f32), j...  216 us
    unnamed x5, local copies, waits for them, and re-layouts  5.31 us

profile of v1, /device:TPU:1, one launch (start us, length us, event | category | flops | bytes accessed | tf_op | source)
XLA Modules:
  0.0 222.0 jit_solution(2795621424775390415)
XLA Ops:
  0.6 1.5 copy.6.mask_ref
  2.2 216.1 %shard_map.59 = (f32[1,512,1024]{2,1,0:T(8,128)}, f32[4,512]{1,0:T(4,128)}) custom-call(f32[1,512,1024]{2,1,0:T(8,128)} %slab.1, f32[512]{0:T(512)} %occ_ref.1, f32[1,512]{1,0:T(1,128)} %bitcast.1, s32[512,2]{1,0:T(8,128)} %copy.6.mask_ref), custom_call_target="tpu_custom_call" | custom-call | tf_op jit(solution)/shard_map/pallas_call | solution.py:355
  218.3 0.0 copy-start
  218.3 3.2 %copy.9 = f32[1,512,1024]{2,1,0:T(8,128)} copy(f32[1,512,1024]{2,1,0:T(8,128)} %get-tuple-element.4) | data formatting | bytes 4194304
  221.4 0.0 copy-done
  221.4 0.6 copy.10
Async XLA Ops:
  218.3 3.2 %copy-start = (f32[4,512]{1,0:T(4,128)S(1)}, f32[4,512]{1,0:T(4,128)}, u32[]{:S(2)}) copy-start(f32[4,512]{1,0:T(4,128)} %get-tuple-element.5) | copy-start | bytes 24580

commit v2 on v1

--- a/solution.py
+++ b/solution.py
@@ -13,6 +13,7 @@
 PIECE = 32
 PIECES = V // PIECE
 PER_BLOCK = BLOCK // PIECE
+WINDOW = 8
 bf16, f32 = jnp.bfloat16, jnp.float32
 
 
@@ -38,8 +39,8 @@
     own_high, own_low, own, other, near, grad, half, vir_col,
     rhs_high, rhs_low, t_high, t_low,
     core_in, x_buf, x_in, y_buf, y_in, z_buf, z_in, last_buf, last_in,
-    local_sem, o_send, o_recv, z_send, z_recv, y_send, y_recv, p_send, p_recv,
-    c_send, c_recv, xs, xr, ys, yr, zs, zr, ls, lr,
+    relay_buf, local_sem, o_send, o_recv, z_send, z_recv, y_send, y_recv, p_send, p_recv,
+    c_send, c_recv, xs, xr, ys, yr, zs, zr, ls, lr, r_send, r_recv,
 ):
     occ, grp = lax.axis_index("occ"), lax.axis_index("grp")
     x, y = lax.rem(occ // 8, 4), lax.rem(occ, 8)
@@ -53,6 +54,13 @@
     has_target = (target >= 0) & (target < 128)
     has_source = (source >= 0) & (source < 128)
     gives_z = z_high == core
+    turn = jnp.where(z_high == 0, 31, 0)
+    is_origin = has_target & (lax.rem(occ, 32) == turn)
+    is_end = has_source & (lax.rem(source, 32) == turn)
+    lane = jnp.where(z_high == 0, y, 7 - y)
+    block_end = (occ // 32) * 32 + 31 - turn
+    block_origin = block_end - step
+    is_relay = (x == jnp.where(z_high == 0, 3, 0)) & (lane >= 1) & (block_origin >= 0) & (block_origin < 128)
 
     load = pltpu.make_async_copy(slab.at[0], own, local_sem.at[0])
     load.start()
@@ -74,7 +82,18 @@
     peers += [(lax.rem(occ + k, 128), grp) for k in (1, 127)]
     for peer in peers:
         pl.semaphore_signal(barrier, inc=1, device_id=peer, device_id_type=MESH)
-    pl.semaphore_wait(barrier, len(peers))
+
+    @pl.when(is_end)
+    def _():
+        for k in range(1, 8):
+            pl.semaphore_signal(barrier, inc=1, device_id=(occ + step * (24 + k), grp), device_id_type=MESH)
+
+    @pl.when(is_relay)
+    def _():
+        pl.semaphore_signal(barrier, inc=1, device_id=(block_origin, grp), device_id_type=MESH)
+
+    extra = is_relay.astype(jnp.int32) + 7 * is_origin.astype(jnp.int32)
+    pl.semaphore_wait(barrier, len(peers) + extra)
 
     def rows(p):
         return pl.ds(pl.multiple_of(p * PIECE, PIECE), PIECE)
@@ -94,6 +113,17 @@
     def y_copy(p):
         return remote(spot(0, p), spot(2, p), y_send.at[p], y_recv.at[p], (target, grp))
 
+    def to_relay(p):
+        return remote(
+            spot(0, p), relay_buf.at[p // 8], y_send.at[p], r_recv.at[p // 8], (occ + step * (25 + lax.rem(p, 8)), grp)
+        )
+
+    def from_relay(turn_number):
+        return remote(
+            relay_buf.at[turn_number], spot(2, turn_number * 8 + lane), r_send.at[turn_number],
+            y_recv.at[turn_number * 8 + lane], (block_end, grp),
+        )
+
     def p_copy(p, kind):
         return remote(spot(kind, p), spot(1, p), p_send.at[p], p_recv.at[p], partner)
 
@@ -103,7 +133,7 @@
         z_copy(p).start()
         return carry
 
-    lax.fori_loop(0, PIECES, start_z, 0)
+    lax.fori_loop(0, WINDOW, start_z, 0)
     o_copy.start()
 
     load.wait()
@@ -148,22 +178,33 @@
         "y": (energy_of(y_index), weight_of(y_index)),
     }
 
-    def block_terms(pieces):
-        width = len(pieces) * BLOCK
-        for n, (ref, _, _) in enumerate(pieces):
-            high, low = split(ref[...])
-            rhs_high[pl.ds(n * BLOCK, BLOCK), :] = high
-            rhs_low[pl.ds(n * BLOCK, BLOCK), :] = low
+    def tiles_of(pieces):
         tiles = []
         for _, number, name in pieces:
             energy, weight = facts[name]
             start = pl.multiple_of(number * BLOCK, BLOCK)
             tiles.append((own_energy + energy - vir_ref[:, pl.ds(start, BLOCK)], weight))
+        return tiles
+
+    def weighted(ref, slot, band, names):
+        parts = [
+            ref[slot, band, n * BLOCK:(n + 1) * BLOCK] * facts[name][1].astype(bf16) for n, name in enumerate(names)
+        ]
+        return parts[0] if len(parts) == 1 else jnp.concatenate(parts, axis=1)
+
+    def amplitudes(slot, pieces):
+        width = len(pieces) * BLOCK
+        names = [name for _, _, name in pieces]
+        for n, (ref, _, _) in enumerate(pieces):
+            high, low = split(ref[...])
+            rhs_high[slot, pl.ds(n * BLOCK, BLOCK), :] = high
+            rhs_low[slot, pl.ds(n * BLOCK, BLOCK), :] = low
+        tiles = tiles_of(pieces)
 
         def rows_of(m, carry):
             band = pl.ds(pl.multiple_of(m * 256, 256), 256)
             left_high, left_low = own_high[band, :], own_low[band, :]
-            right_high, right_low = rhs_high[:width, :], rhs_low[:width, :]
+            right_high, right_low = rhs_high[slot, :width, :], rhs_low[slot, :width, :]
             coulomb = times_t(left_high, right_high)
             coulomb += times_t(left_high, right_low)
             coulomb += times_t(left_low, right_high)
@@ -171,53 +212,51 @@
             for n, (base, _) in enumerate(tiles):
                 cut = slice(n * BLOCK, (n + 1) * BLOCK)
                 high, low = split(coulomb[:, cut] / (base - column))
-                t_high[band, cut] = high
-                t_low[band, cut] = low
-            weighted_high = jnp.concatenate(
-                [t_high[band, n * BLOCK:(n + 1) * BLOCK] * tiles[n][1].astype(bf16) for n in range(len(tiles))], axis=1
-            )
-            weighted_low = jnp.concatenate(
-                [t_low[band, n * BLOCK:(n + 1) * BLOCK] * tiles[n][1].astype(bf16) for n in range(len(tiles))], axis=1
-            )
-            grad[band, :] += (
-                times(weighted_high, right_high) + times(weighted_high, right_low) + times(weighted_low, right_high)
-            )
+                t_high[slot, band, cut] = high
+                t_low[slot, band, cut] = low
             return carry
 
         lax.fori_loop(0, 2, rows_of, 0)
 
         def density_rows(m, carry):
             band = pl.ds(pl.multiple_of(m * 256, 256), 256)
-            weighted_high = jnp.concatenate(
-                [t_high[band, n * BLOCK:(n + 1) * BLOCK] * tiles[n][1].astype(bf16) for n in range(len(tiles))], axis=1
-            )
-            weighted_low = jnp.concatenate(
-                [t_low[band, n * BLOCK:(n + 1) * BLOCK] * tiles[n][1].astype(bf16) for n in range(len(tiles))], axis=1
-            )
+            left_high, left_low = weighted(t_high, slot, band, names), weighted(t_low, slot, band, names)
             for h in range(2):
-                other_high = t_high[pl.ds(h * 256, 256), :width]
-                other_low = t_low[pl.ds(h * 256, 256), :width]
+                other_high = t_high[slot, pl.ds(h * 256, 256), :width]
+                other_low = t_low[slot, pl.ds(h * 256, 256), :width]
                 half[h, band, :] += (
-                    times_t(weighted_high, other_high)
-                    + times_t(weighted_high, other_low)
-                    + times_t(weighted_low, other_high)
+                    times_t(left_high, other_high) + times_t(left_high, other_low) + times_t(left_low, other_high)
                 )
             return carry
 
         lax.fori_loop(0, 2, density_rows, 0)
 
+    def gradient(slot, names):
+        width = len(names) * BLOCK
+
+        def rows_of(m, carry):
+            band = pl.ds(pl.multiple_of(m * 256, 256), 256)
+            left_high, left_low = weighted(t_high, slot, band, names), weighted(t_low, slot, band, names)
+            right_high, right_low = rhs_high[slot, :width, :], rhs_low[slot, :width, :]
+            grad[band, :] += times(left_high, right_high) + times(left_high, right_low) + times(left_low, right_high)
+            return carry
+
+        lax.fori_loop(0, 2, rows_of, 0)
+
     def part(ref, b):
         return ref.at[pl.ds(pl.multiple_of(b * BLOCK, BLOCK), BLOCK)]
 
     def own_blocks(b, carry):
-        block_terms([(part(own, 2 * b), 2 * b, "own"), (part(own, 2 * b + 1), 2 * b + 1, "own")])
+        amplitudes(4, [(part(own, 2 * b), 2 * b, "own"), (part(own, 2 * b + 1), 2 * b + 1, "own")])
+        gradient(4, ["own", "own"])
         return carry
 
     lax.fori_loop(0, 2, own_blocks, 0)
     o_copy.wait_recv()
 
     def other_blocks(b, carry):
-        block_terms([(part(other, 2 * b), 2 * b, "o"), (part(other, 2 * b + 1), 2 * b + 1, "o")])
+        amplitudes(4, [(part(other, 2 * b), 2 * b, "o"), (part(other, 2 * b + 1), 2 * b + 1, "o")])
+        gradient(4, ["o", "o"])
         return carry
 
     lax.fori_loop(0, 2, other_blocks, 0)
@@ -225,13 +264,24 @@
     def take(p, carry):
         z_copy(p).wait_recv()
 
-        @pl.when(has_target)
+        relayed = is_origin & (lax.rem(p, 8) != 0)
+
+        @pl.when(has_target & jnp.logical_not(relayed))
         def _():
             y_copy(p).start()
 
+        @pl.when(relayed)
+        def _():
+            to_relay(p).start()
+
         @pl.when(gives_z)
         def _():
             p_copy(p, 0).start()
+
+        @pl.when(p + WINDOW < PIECES)
+        def _():
+            z_copy(p).wait_send()
+            z_copy(p + WINDOW).start()
 
         return carry
 
@@ -246,29 +296,52 @@
 
         return carry
 
+    def over(b, step_of):
+        lax.fori_loop(b * PER_BLOCK, (b + 1) * PER_BLOCK, step_of, 0)
+
+    def settle(p, carry):
+        @pl.when(has_source | jnp.logical_not(gives_z))
+        def _():
+            p_copy(p, 0).wait_recv()
+
+        return carry
+
+    over(0, take)
+
+    def hand_on(h):
+        to_relay(h * 8).wait_recv()
+        from_relay(h).start()
+
     def near_blocks(b, carry):
-        lax.fori_loop(b * PER_BLOCK, (b + 1) * PER_BLOCK, take, 0)
-        lax.fori_loop(b * PER_BLOCK, (b + 1) * PER_BLOCK, pass_on, 0)
-
-        def settle(p, carry):
-            @pl.when(has_source | jnp.logical_not(gives_z))
-            def _():
-                p_copy(p, 0).wait_recv()
-
-            return carry
-
-        lax.fori_loop(b * PER_BLOCK, (b + 1) * PER_BLOCK, settle, 0)
-        block_terms(
-            [(part(near, 3 * b), b, "z"), (part(near, 3 * b + 1), b, "p"), (part(near, 3 * b + 2), b, "y")]
-        )
+        amplitudes(4, [(part(near, 3 * b), b, "z")])
+        gradient(4, ["z"])
+
+        @pl.when(is_relay & (lane < 4) & (b == 2))
+        def _():
+            hand_on(1)
+
+        @pl.when(b < 3)
+        def _():
+            over(b + 1, take)
+
+        @pl.when(is_relay & (((b == 0) & (lane < 4)) | ((b == 1) & (lane >= 4))))
+        def _():
+            hand_on(0)
+
+        @pl.when(is_relay & (lane >= 4) & (b == 2))
+        def _():
+            hand_on(1)
+
+        over(b, pass_on)
+        over(b, settle)
+        amplitudes(b, [(part(near, 3 * b + 1), b, "p"), (part(near, 3 * b + 2), b, "y")])
         return carry
 
     lax.fori_loop(0, 4, near_blocks, 0)
-    save = pltpu.make_async_copy(grad, grad_out.at[0], local_sem.at[1])
-    save.start()
 
     c_copy = remote(half.at[1 - core], core_in, c_send, c_recv, partner)
     c_copy.start()
+    gradient(0, ["p", "y"])
     c_copy.wait_recv()
     for q in range(4):
         for k in range(4):
@@ -279,6 +352,8 @@
     ]
     for copy in x_copies:
         copy.start()
+    gradient(1, ["p", "y"])
+    gradient(2, ["p", "y"])
     for copy in x_copies:
         copy.wait_recv()
     for q in range(4):
@@ -291,6 +366,9 @@
     ]
     for copy in y_copies:
         copy.start()
+    gradient(3, ["p", "y"])
+    save = pltpu.make_async_copy(grad, grad_out.at[0], local_sem.at[1])
+    save.start()
     for copy in y_copies:
         copy.wait_recv()
     total = y_buf[y]
@@ -327,8 +405,15 @@
 
     o_copy.wait_send()
 
+    @pl.when(is_relay)
+    def _():
+        for h in range(2):
+            from_relay(h).wait_send()
+
     def drain(p, carry):
-        z_copy(p).wait_send()
+        @pl.when(p + WINDOW >= PIECES)
+        def _():
+            z_copy(p).wait_send()
 
         @pl.when(has_target)
         def _():
@@ -360,16 +445,17 @@
         scratch_shapes=[
             vmem((V, A), bf16), vmem((V, A), bf16), vmem((V, A), f32), vmem((V, A), f32),
             vmem((12 * BLOCK, A), f32), vmem((V, A), f32), vmem((2, V, V // 2), f32), vmem((V, 128), f32),
-            vmem((3 * BLOCK, A), bf16), vmem((3 * BLOCK, A), bf16),
-            vmem((V, 3 * BLOCK), bf16), vmem((V, 3 * BLOCK), bf16),
+            vmem((5, 2 * BLOCK, A), bf16), vmem((5, 2 * BLOCK, A), bf16),
+            vmem((5, V, 2 * BLOCK), bf16), vmem((5, V, 2 * BLOCK), bf16),
             vmem((V, 256), f32), vmem((4, 128, 256), f32), vmem((3, 128, 256), f32),
             vmem((8, 16, 256), f32), vmem((7, 16, 256), f32), vmem((4, 8, 256), f32), vmem((7, 8, 256), f32),
-            vmem((8, 256), f32), vmem((8, 256), f32),
+            vmem((8, 256), f32), vmem((8, 256), f32), vmem((2, PIECE, A), f32),
             dma((2,)), dma, dma, dma((PIECES,)), dma((PIECES,)), dma((PIECES,)), dma((PIECES,)), dma((PIECES,)),
             dma((PIECES,)), dma, dma, dma((3,)), dma((3,)), dma((7,)), dma((7,)), dma((7,)), dma((7,)), dma, dma,
+            dma((2,)), dma((2,)),
         ],
         compiler_params=pltpu.CompilerParams(
-            collective_id=0, has_side_effects=True, vmem_limit_bytes=60 * 1024 * 1024
+            collective_id=0, has_side_effects=True, vmem_limit_bytes=34 * 1024 * 1024
         ),
     )(slabs, occ_energy, vir_energy[None, :], pair_mask)
 

time: 222 us -> 184 us (0.83)
  Pallas kernels: 216 us -> 177 us
    pallas_call x1, Pallas kernels: 216 us -> 177 us  [body(): pl.pallas_call(kernel, out_shape=(jax.ShapeDtypeStruct((1, V, A), f32), j...]
    unnamed x5 -> x9, local copies, waits for them, and re-layouts: 5.31 us -> 5.7 us
where the time goes in v2:
time: 184 us; the launch traced here: 183 us
  Pallas kernels  177 us (96%)
  local copies, waits for them, and re-layouts  5.7 us (3%)
    pallas_call x1, Pallas kernels, body(): pl.pallas_call(kernel, out_shape=(jax.ShapeDtypeStruct((1, V, A), f32), j...  177 us
    unnamed x9, local copies, waits for them, and re-layouts  5.7 us

profile of v2, /device:TPU:1, one launch (start us, length us, event | category | flops | bytes accessed | tf_op | source)
XLA Modules:
  0.0 182.9 jit_solution(3511048667515332416)
XLA Ops:
  0.6 0.8 copy.6.mask_ref
  1.5 0.0 copy-start
  1.5 1.6 copy-done
  3.1 0.0 copy-start.1
  3.1 0.7 copy-done.1
  3.7 0.0 copy-start.2
  3.7 0.7 copy-done.2
  4.4 176.6 %shard_map.59 = (f32[1,512,1024]{2,1,0:T(8,128)S(1)}, f32[4,512]{1,0:T(4,128)S(1)}) custom-call(f32[1,512,1024]{2,1,0:T(8,128)S(1)} %copy-done, f32[512]{0:T(512)S(1)} %copy-done.1, f32[1,512]{1,0:T(1,128)S(1)} %bitcast.1, s32[512,2]{1,0:T(8,128)S(1)} %copy.6.mask_ref), custom_call_target="tpu_custom_call" | custom-call | tf_op jit(solution)/shard_map/pallas_call | solution.py:440
  181.0 1.3 copy.9
  182.3 0.6 copy.10
Async XLA Ops:
  1.5 1.6 copy-start
  3.1 0.7 copy-start.1
  3.7 0.7 copy-start.2
